TPU v7x, 32 devices: a whole 2x2x4 slice. The times are simulated.
32 devices in a mesh: fsdp: 8 (over z, x), mat: 4 (over y, core).
Axes of the slice: x: 2, y: 2, z: 4, core: 2. Of those that a mesh axis runs over, the one named last changes fastest.
Arguments:
- grads: bfloat16 [4, 8192, 16384], P('mat', 'fsdp'), may hold values from -5000 to 5000
- p_old: bfloat16 [4, 8192, 256], P('mat', 'fsdp'), may hold values from -2 to 2
- p_new: bfloat16 [4, 8192, 256], P('mat', 'fsdp'), may hold values from -2 to 2
- m_old: float32 [4, 16384, 256], P('mat', 'fsdp'), may hold values from -4 to 4
- v_old: float32 [4, 16384, 256], P('mat', 'fsdp'), may hold values from 0.003 to 0.03
Outputs:
- update: bfloat16 [4, 8192, 16384], P('mat', 'fsdp')
- m_new: float32 [4, 16384, 256], P('mat', 'fsdp')
- v_new: float32 [4, 16384, 256], P('mat', 'fsdp')
All inputs are finite; a program needn't handle non-finite values.
Results may differ from a plain program's by a relative error of at most 0.0046.
Values may be sent and summed in bfloat16 or wider, within the bound.
A program may use at most 320 MiB of HBM per device.

v0:
```python
import jax
import jax.numpy as jnp
from jax import lax
from jax.sharding import PartitionSpec as P

D = 8192
COLS = 16384


def shards(grads, p_old, p_new, m_old, v_old):
    grad = grads[0]
    basis_old = p_old[0]
    basis_new = p_new[0]
    first_old = m_old[0]
    second_old = v_old[0]
    total = lax.psum(jnp.sum(jnp.square(grad.astype(jnp.float32))), ("fsdp", "mat"))
    mat_count = lax.axis_size("mat")
    clip = jnp.minimum(1.0, 0.5 / jnp.sqrt(total / (mat_count * D * COLS) + 1e-06))
    partial_gram = lax.dot_general(
        basis_new, basis_old, (((0,), (0,)), ((), ())), preferred_element_type=jnp.float32
    )
    gram = lax.psum(partial_gram, "fsdp")
    rot_m = jnp.dot(first_old, gram.T, precision=lax.Precision.HIGHEST)
    rot_v = jnp.dot(second_old, (gram * gram).T, precision=lax.Precision.HIGHEST)
    proj = clip * lax.psum_scatter(
        lax.dot_general(
            grad, basis_new, (((0,), (0,)), ((), ())), preferred_element_type=jnp.float32
        ),
        "fsdp",
        scatter_dimension=0,
        tiled=True,
    )
    first = 0.9 * rot_m + 0.1 * proj
    second = 0.99 * rot_v + 0.01 * proj * proj
    dirn = (first / (jnp.sqrt(second) + 1e-08)).astype(jnp.bfloat16)
    upd = lax.dot_general(
        basis_new,
        lax.all_gather(dirn, "fsdp", axis=0, tiled=True),
        (((1,), (1,)), ((), ())),
        preferred_element_type=jnp.float32,
    ).astype(jnp.bfloat16)
    return (upd[None], first[None], second[None])


def solution(mesh):
    placed = (
        P("mat", "fsdp", None),
        P("mat", "fsdp", None),
        P("mat", "fsdp", None),
        P("mat", "fsdp", None),
        P("mat", "fsdp", None),
    )
    return jax.shard_map(
        shards,
        mesh=mesh,
        in_specs=placed,
        out_specs=(P("mat", "fsdp", None), P("mat", "fsdp", None), P("mat", "fsdp", None)),
        check_vma=False,
    )
```

profile of v0, /device:TPU:0, one launch (start us, length us, event | category | flops | bytes accessed | tf_op | source)
XLA Modules:
  0.0 569.8 jit_solution(3575329393713956755)
XLA Ops:
  7.2 0.0 copy-start
  7.2 0.0 all-reduce.2.cloned.1.call-start
  7.2 2.4 fusion.8
  9.6 0.0 all-reduce.2.cloned.1.call-update
  9.6 0.0 reduce-scatter.2.cloned.1.call-start
  9.7 18.8 %fusion = f32[16384,256]{0,1:T(8,128)} fusion(bf16[1,1024,16384]{2,1,0:T(8,128)(2,1)} %param.5, bf16[1,1024,256]{2,1,0:T(8,128)(2,1)} %param.7), kind=kOutput, calls=%fused_computation.1 | convolution fusion | flops 8589934592 | bytes 50855936 | tf_op jit(solution)/shard_map/dot_general | solution.py:26
  28.5 0.0 reduce-scatter.2.cloned.1.call-update
  28.6 0.0 all-gather.2.cloned.1.call-start
  28.6 19.6 %multiply_reduce_fusion = f32[]{:T(128)} fusion(bf16[1,1024,16384]{2,1,0:T(8,128)(2,1)} %param.5), kind=kLoop, calls=%fused_computation | loop fusion | flops 50331648 | bytes 33554436 | tf_op jit(solution)/shard_map/reduce_sum | solution.py:16
  48.2 42.4 %psum.15 = f32[]{:T(128)} all-reduce(f32[]{:T(128)} %multiply_reduce_fusion), channel_id=1, replica_groups=mesh['fsdp'=8,'mat'=4] {'fsdp','mat'}, use_global_device_ids=true, to_apply=%region_2.0 | all-reduce | flops 1 | bytes 8 | tf_op jit(solution)/shard_map/psum | solution.py:16
  91.3 0.0 all-reduce.2.cloned.1.call-done
  91.3 0.0 copy-start.6
  91.3 277.4 %reduce-scatter.2.cloned.1.call-done = f32[2048,256]{0,1:T(8,128)} async-done(((f32[16384,256]{0,1:T(8,128)}), f32[2048,256]{0,1:T(8,128)}) %reduce-scatter.2.cloned.1.call-update) | async-done | bytes 2097168 | tf_op jit(solution)/shard_map/reduce_scatter | solution.py:25
  368.8 0.0 copy-start.5
  368.8 4.6 fusion.3
  373.4 0.0 copy-done
  373.4 0.0 copy-done.6
  373.4 0.0 copy-done.5
  373.4 0.0 copy-start.2
  373.4 4.5 divide_convert_fusion
  377.9 0.0 copy-done.2
  377.9 0.0 all-gather.2.cloned.1.call-update
  378.0 0.0 copy-start.3
  378.0 3.0 copy.10
  381.0 0.0 copy-done.3
  381.0 0.0 copy-start.4
  381.0 1.8 copy.11
  382.8 118.8 %all-gather.2.cloned.1.call-done = bf16[16384,256]{0,1:T(8,128)(2,1)} async-done(((bf16[2048,256]{0,1:T(8,128)(2,1)}), bf16[16384,256]{0,1:T(8,128)(2,1)}) %all-gather.2.cloned.1.call-update) | async-done | bytes 8388624 | tf_op jit(solution)/shard_map/all_gather | solution.py:38
  501.7 0.0 copy-done.4
  501.7 17.5 %convert_bitcast_fusion = bf16[1,1024,16384]{1,2,0:T(8,128)(2,1)} fusion(bf16[16384,256]{0,1:T(8,128)(2,1)} %all-gather.2.cloned.1.call-done, bf16[1,1024,256]{2,1,0:T(8,128)(2,1)S(1)} %copy-done.4), kind=kOutput, calls=%fused_computation.3 | convolution fusion | flops 8606711808 | bytes 42467328 | tf_op jit(solution)/shard_map/dot_general | solution.py:36
  519.2 44.0 %copy.9 = bf16[1,1024,16384]{2,1,0:T(8,128)(2,1)} copy(bf16[1,1024,16384]{1,2,0:T(8,128)(2,1)} %convert_bitcast_fusion) | data formatting | bytes 67108864
  563.2 0.0 copy-done.1
  (1 shorter events, 0.0 us)
Async XLA Ops:
  7.2 366.2 %copy-start = (f32[1,2048,256]{2,1,0:T(8,128)S(1)}, f32[1,2048,256]{2,1,0:T(8,128)}, u32[]{:S(2)}) copy-start(f32[1,2048,256]{2,1,0:T(8,128)} %param.8) | copy-start | bytes 6291460
  7.2 84.1 %all-reduce.2.cloned.1.call-start = ((), (), s32[]{:S(2)}) async-start(), calls=%async_computation.1 | async-start | bytes 524288 | tf_op jit(solution)/shard_map/psum | solution.py:22
  9.6 359.1 %reduce-scatter.2.cloned.1.call-start = ((), (), s32[]{:S(2)}) async-start(), calls=%async_computation.2 | async-start | bytes 18874368 | tf_op jit(solution)/shard_map/reduce_scatter | solution.py:25
  28.6 473.1 %all-gather.2.cloned.1.call-start = ((), (), s32[]{:S(2)}) async-start(), calls=%async_computation.3 | async-start | bytes 9437184 | tf_op jit(solution)/shard_map/all_gather | solution.py:38
  91.3 282.1 %copy-start.6 = (f32[256,256]{1,0:T(8,128)S(1)}, f32[256,256]{1,0:T(8,128)}, u32[]{:S(2)}) copy-start(f32[256,256]{1,0:T(8,128)} %all-reduce.2.cloned.1.call-done) | copy-start | bytes 786436
  368.8 4.7 copy-start.5
  373.4 4.5 copy-start.2
  378.0 3.0 copy-start.3
  381.0 120.7 %copy-start.4 = (bf16[1,1024,256]{2,1,0:T(8,128)(2,1)S(1)}, bf16[1,1024,256]{2,1,0:T(8,128)(2,1)}, u32[]{:S(2)}) copy-start(bf16[1,1024,256]{2,1,0:T(8,128)(2,1)} %param.7) | copy-start | bytes 1572868
  519.2 44.0 %copy-start.1 = (f32[1,2048,256]{2,1,0:T(8,128)S(1)}, f32[1,2048,256]{2,1,0:T(8,128)}, u32[]{:S(2)}) copy-start(f32[1,2048,256]{2,1,0:T(8,128)} %param.8) | copy-start | bytes 6291460
Sparse Core Ops, SparseCore 0:
  11.9 73.7 all-reduce.1
  90.1 278.6 reduce-scatter.1
  378.1 123.5 all-gather.1
where the time goes:
time: 571 us; the launch traced here: 570 us
  waiting for transfers between devices  396 us (69%)
  local copies, waits for them, and re-layouts  48.9 us (9%)
  matrix products  47.9 us (8%)
  blocking collectives  42.4 us (7%)
  other arithmetic  19.6 us (3%)
  between operations  14.5 us (3%)
    reduce_scatter x1, waiting for transfers between devices, shards(): lax.psum_scatter(lax.dot_general(grad, basis_new, (((0,), (0,)), ((), ())...  277 us
    all_gather x1, waiting for transfers between devices, shards(): lax.all_gather(dirn, 'fsdp', axis=0, tiled=True)  119 us
    unnamed x17, local copies, waits for them, and re-layouts  48.9 us
    psum x1, blocking collectives, shards(): lax.psum(jnp.sum(jnp.square(grad.astype(jnp.float32))), ('fsdp', 'mat'))  42.4 us
    reduce_sum x1, other arithmetic, shards(): jnp.sum(jnp.square(grad.astype(jnp.float32)))  19.6 us
    dot_general x1, matrix products, shards(): lax.dot_general(grad, basis_new, (((0,), (0,)), ((), ())), preferred_elem...  18.8 us
    dot_general x1, matrix products, shards(): lax.dot_general(basis_new, lax.all_gather(dirn, 'fsdp', axis=0, tiled=Tru...  17.5 us
  transfers between devices with their start and end apart: 3, of which 2 were waited for; matrix products, arithmetic and copies ran while one was open for 8% of the time, Pallas kernels for 0%

commit v1 on v0

--- a/solution.py
+++ b/solution.py
@@ -5,6 +5,18 @@
 
 D = 8192
 COLS = 16384
+
+
+def doubled_up(value, axis, dim):
+    ways, here = (lax.axis_size(axis), lax.axis_index(axis))
+    grown, reach = (value, 1)
+    while reach < ways:
+        theirs = lax.ppermute(grown, axis, [(d, d ^ reach) for d in range(ways)])
+        mine_first = jnp.concatenate([grown, theirs], axis=dim)
+        theirs_first = jnp.concatenate([theirs, grown], axis=dim)
+        grown = jnp.where(here & reach == 0, mine_first, theirs_first)
+        reach = 2 * reach
+    return grown
 
 
 def shards(grads, p_old, p_new, m_old, v_old):
@@ -35,7 +47,7 @@
     dirn = (first / (jnp.sqrt(second) + 1e-08)).astype(jnp.bfloat16)
     upd = lax.dot_general(
         basis_new,
-        lax.all_gather(dirn, "fsdp", axis=0, tiled=True),
+        doubled_up(dirn, "fsdp", 0),
         (((1,), (1,)), ((), ())),
         preferred_element_type=jnp.float32,
     ).astype(jnp.bfloat16)

time: 571 us -> 713 us (1.25)
  waiting for transfers between devices: 396 us -> 521 us
    ppermute x0 -> x3, waiting for transfers between devices: none -> 243 us  [doubled_up(): theirs = lax.ppermute(grown, axis, [(d, d ^ reach) for d in range(ways)])]
    all_gather x1 -> x0, waiting for transfers between devices: 119 us -> none  [shards(): lax.all_gather(dirn, 'fsdp', axis=0, tiled=True)]
  transfers between devices with their start and end apart: 3 -> 5, of which waited for: 2 -> 4; matrix products, arithmetic and copies ran while one was open for 8% -> 6% of each run, Pallas kernels for 0% -> 0%
where the time goes in v1:
time: 713 us; the launch traced here: 711 us
  waiting for transfers between devices  521 us (73%)
  matrix products  53.1 us (7%)
  local copies, waits for them, and re-layouts  48.8 us (7%)
  blocking collectives  42.5 us (6%)
  other arithmetic  26.6 us (4%)
  between operations  14.8 us (2%)
    reduce_scatter x1, waiting for transfers between devices, shards(): lax.psum_scatter(lax.dot_general(grad, basis_new, (((0,), (0,)), ((), ())...  278 us
    ppermute x3, waiting for transfers between devices, doubled_up(): theirs = lax.ppermute(grown, axis, [(d, d ^ reach) for d in range(ways)])  243 us
    unnamed x17, local copies, waits for them, and re-layouts  48.8 us
    psum x1, blocking collectives, shards(): lax.psum(jnp.sum(jnp.square(grad.astype(jnp.float32))), ('fsdp', 'mat'))  42.5 us
    dot_general x1, matrix products, shards(): lax.dot_general(basis_new, doubled_up(dirn, 'fsdp', 0), (((1,), (1,)), ((...  23.1 us
    reduce_sum x1, other arithmetic, shards(): jnp.sum(jnp.square(grad.astype(jnp.float32)))  19.6 us
    dot_general x1, matrix products, shards(): lax.dot_general(grad, basis_new, (((0,), (0,)), ((), ())), preferred_elem...  18.8 us
  transfers between devices with their start and end apart: 5, of which 4 were waited for; matrix products, arithmetic and copies ran while one was open for 6% of the time, Pallas kernels for 0%

profile of v1, /device:TPU:0, one launch (start us, length us, event | category | flops | bytes accessed | tf_op | source)
XLA Modules:
  0.0 711.2 jit_solution(4851754070093124563)
XLA Ops:
  7.2 0.0 copy-start
  7.2 0.0 all-reduce.2.cloned.1.call-start
  7.2 2.4 fusion.14
  9.6 0.0 all-reduce.2.cloned.1.call-update
  9.6 0.0 reduce-scatter.2.cloned.1.call-start
  9.7 18.8 %fusion = f32[16384,256]{0,1:T(8,128)} fusion(bf16[1,1024,16384]{2,1,0:T(8,128)(2,1)} %param.5, bf16[1,1024,256]{2,1,0:T(8,128)(2,1)} %param.7), kind=kOutput, calls=%fused_computation.1 | convolution fusion | flops 8589934592 | bytes 50855936 | tf_op jit(solution)/shard_map/dot_general | solution.py:38
  28.5 0.0 reduce-scatter.2.cloned.1.call-update
  28.6 19.6 %multiply_reduce_fusion = f32[]{:T(128)} fusion(bf16[1,1024,16384]{2,1,0:T(8,128)(2,1)} %param.5), kind=kLoop, calls=%fused_computation | loop fusion | flops 50331648 | bytes 33554436 | tf_op jit(solution)/shard_map/reduce_sum | solution.py:28
  48.1 42.5 %psum.15 = f32[]{:T(128)} all-reduce(f32[]{:T(128)} %multiply_reduce_fusion), channel_id=1, replica_groups=mesh['fsdp'=8,'mat'=4] {'fsdp','mat'}, use_global_device_ids=true, to_apply=%region_2.0 | all-reduce | flops 1 | bytes 8 | tf_op jit(solution)/shard_map/psum | solution.py:28
  91.3 0.0 all-reduce.2.cloned.1.call-done
  91.3 0.0 copy-start.6
  91.3 277.5 %reduce-scatter.2.cloned.1.call-done = f32[2048,256]{0,1:T(8,128)} async-done(((f32[16384,256]{0,1:T(8,128)}), f32[2048,256]{0,1:T(8,128)}) %reduce-scatter.2.cloned.1.call-update) | async-done | bytes 2097168 | tf_op jit(solution)/shard_map/reduce_scatter | solution.py:37
  368.8 4.6 fusion.9
  373.5 0.0 copy-done
  373.5 0.0 copy-done.6
  373.5 0.0 copy-done.4
  373.5 0.0 copy-start.2
  373.5 4.1 divide_convert_fusion
  377.6 0.0 copy-done.2
  377.6 1.5 collective-permute-start
  379.1 23.3 %collective-permute-done = bf16[2048,256]{0,1:T(8,128)(2,1)} collective-permute-done((bf16[2048,256]{0,1:T(8,128)(2,1)S(1)}, bf16[2048,256]{0,1:T(8,128)(2,1)}, u32[]{:S(2)}, u32[]{:S(2)}) %collective-permute-start) | collective-permute-done | bytes 1048608 | tf_op jit(solution)/shard_map/ppermute | solution.py:14
  402.3 2.4 maximum_select_fusion.3
  404.7 0.9 collective-permute-start.1
  405.6 45.5 %collective-permute-done.1 = bf16[4096,256]{0,1:T(8,128)(2,1)} collective-permute-done((bf16[4096,256]{0,1:T(8,128)(2,1)S(1)}, bf16[4096,256]{0,1:T(8,128)(2,1)}, u32[]{:S(2)}, u32[]{:S(2)}) %collective-permute-start.1) | collective-permute-done | bytes 2097184 | tf_op jit(solution)/shard_map/ppermute | solution.py:14
  451.1 4.7 maximum_select_fusion.2
  455.8 2.2 collective-permute-start.2
  458.0 2.9 copy.10
  460.9 1.8 copy.11
  462.7 174.5 %collective-permute-done.2 = bf16[8192,256]{0,1:T(8,128)(2,1)} collective-permute-done((bf16[8192,256]{0,1:T(8,128)(2,1)}, bf16[8192,256]{0,1:T(8,128)(2,1)}, u32[]{:S(2)}, u32[]{:S(2)}) %collective-permute-start.2) | collective-permute-done | bytes 4194336 | tf_op jit(solution)/shard_map/ppermute | solution.py:14
  637.2 23.1 %convert_bitcast_fusion = bf16[1,1024,16384]{1,2,0:T(8,128)(2,1)} fusion(bf16[8192,256]{0,1:T(8,128)(2,1)} %collective-permute-done.2, bf16[8192,256]{0,1:T(8,128)(2,1)} %maximum_select_fusion.2, pred[]{:T(512)S(6)} %eq.9, bf16[1,1024,256]{2,1,0:T(8,128)(2,1)S(1)} %copy-done.5), kind=kOutput, calls=%fused_computation.3 | convolution fusion | flops 8644460544 | bytes 42467328 | tf_op jit(solution)/shard_map/dot_general | solution.py:48
  660.3 44.0 %copy.9 = bf16[1,1024,16384]{2,1,0:T(8,128)(2,1)} copy(bf16[1,1024,16384]{1,2,0:T(8,128)(2,1)} %convert_bitcast_fusion) | data formatting | bytes 67108864
  704.4 0.0 copy-done.1
  (6 shorter events, 0.0 us)
Async XLA Ops:
  7.2 366.3 %copy-start = (f32[1,2048,256]{2,1,0:T(8,128)S(1)}, f32[1,2048,256]{2,1,0:T(8,128)}, u32[]{:S(2)}) copy-start(f32[1,2048,256]{2,1,0:T(8,128)} %param.8) | copy-start | bytes 6291460
  7.2 84.1 %all-reduce.2.cloned.1.call-start = ((), (), s32[]{:S(2)}) async-start(), calls=%async_computation.1 | async-start | bytes 524288 | tf_op jit(solution)/shard_map/psum | solution.py:34
  9.6 359.2 %reduce-scatter.2.cloned.1.call-start = ((), (), s32[]{:S(2)}) async-start(), calls=%async_computation.2 | async-start | bytes 18874368 | tf_op jit(solution)/shard_map/reduce_scatter | solution.py:37
  91.3 282.2 %copy-start.6 = (f32[256,256]{1,0:T(8,128)S(1)}, f32[256,256]{1,0:T(8,128)}, u32[]{:S(2)}) copy-start(f32[256,256]{1,0:T(8,128)} %all-reduce.2.cloned.1.call-done) | copy-start | bytes 786436
  368.8 4.7 copy-start.4
  373.5 4.2 copy-start.2
  377.6 24.7 %collective-permute-start = (bf16[2048,256]{0,1:T(8,128)(2,1)S(1)}, bf16[2048,256]{0,1:T(8,128)(2,1)}, u32[]{:S(2)}, u32[]{:S(2)}) collective-permute-start(bf16[2048,256]{0,1:T(8,128)(2,1)S(1)} %get-tuple-element.6), channel_id=1, source_target_pairs={{0,4},{4,0},{8,12},{12,8},{16,20},{20,16},{24,28},{28,24},{1,5},{5... | collective-permute-start | bytes 3145736 | tf_op jit(solution)/shard_map/ppermute | solution.py:14
  404.7 46.4 %collective-permute-start.1 = (bf16[4096,256]{0,1:T(8,128)(2,1)S(1)}, bf16[4096,256]{0,1:T(8,128)(2,1)}, u32[]{:S(2)}, u32[]{:S(2)}) collective-permute-start(bf16[4096,256]{0,1:T(8,128)(2,1)S(1)} %maximum_select_fusion.3), channel_id=1, source_target_pairs={{0,8},{4,12},{8,0},{12,4},{16,24},{20,28},{24,16},{28,20},{1,9},{5... | collective-permute-start | bytes 6291464 | tf_op jit(solution)/shard_map/ppermute | solution.py:14
  455.8 5.1 copy-start.3
  455.8 181.4 %collective-permute-start.2 = (bf16[8192,256]{0,1:T(8,128)(2,1)}, bf16[8192,256]{0,1:T(8,128)(2,1)}, u32[]{:S(2)}, u32[]{:S(2)}) collective-permute-start(bf16[8192,256]{0,1:T(8,128)(2,1)} %maximum_select_fusion.2), channel_id=1, source_target_pairs={{0,16},{4,20},{8,24},{12,28},{16,0},{20,4},{24,8},{28,12},{1,17},{... | collective-permute-start | bytes 12582920 | tf_op jit(solution)/shard_map/ppermute | solution.py:14
  458.0 179.2 %copy-start.5 = (bf16[1,1024,256]{2,1,0:T(8,128)(2,1)S(1)}, bf16[1,1024,256]{2,1,0:T(8,128)(2,1)}, u32[]{:S(2)}) copy-start(bf16[1,1024,256]{2,1,0:T(8,128)(2,1)} %param.7) | copy-start | bytes 1572868
  660.3 44.1 %copy-start.1 = (f32[1,2048,256]{2,1,0:T(8,128)S(1)}, f32[1,2048,256]{2,1,0:T(8,128)}, u32[]{:S(2)}) copy-start(f32[1,2048,256]{2,1,0:T(8,128)} %param.8) | copy-start | bytes 6291460
Sparse Core Ops, SparseCore 0:
  11.9 73.7 all-reduce.1
  90.1 278.7 reduce-scatter.1
